TPU v7x, 512 devices: a whole 4x4x16 slice. The times are simulated.
512 devices in a mesh: row: 16 (over y, z_hi), col: 32 (over x, z_lo, core).
Axes of the slice: x: 4, y: 4, z: 16 (z_hi: 4, z_lo: 4; z = z_hi * 4 + z_lo), core: 2. Of those that a mesh axis runs over, the one named last changes fastest.
Arguments:
- inv_known: float32 [8192, 8192], P('row', 'col'), as said below
- pattern: int32 [128, 128], P('row', 'col'), may hold values from 0 to 1, as said below
- factor: float32 [8192, 2, 512], P(('row', 'col')), may hold values from -0.0625 to 0.0625
- listed: int32 [8192, 2], P(('row', 'col')), may hold values 0 or 1
- diag_inverse: float32 [512, 2, 512], P('col'), may hold values from -6 to 6
Outputs:
- inverse_columns: float32 [512, 2, 8192], P('col', None, 'row')
- schur: float32 [512, 2, 512], P('col')
Inputs may be any that keep to these rules, and one draw needn't show every extreme that they name: `inv_known`: symmetric. `pattern`: symmetric; every diagonal tile is present.
All inputs are finite; a program needn't handle non-finite values. No bound on the sum of `listed` on one device may be relied on, other than what follows from the above.
Results may differ from a plain program's by a relative error of at most 0.0001.
Values sent between devices are 32-bit elements; how exact they have to be, the bound alone decides.
A program may use at most 64 MiB of HBM per device.

v0:
```python
import jax
import jax.numpy as jnp
from jax import lax
from jax.sharding import PartitionSpec as P


def in_one_piece(arrays, axis, dim, along):
    columns = [a.reshape(*a.shape[:along], -1) for a in arrays]
    both = jnp.concatenate(columns, axis=along)
    filled, at, finished = (lax.all_gather(both, axis, axis=dim, tiled=True), 0, [])
    for a, column in zip(arrays, columns):
        slab = filled[..., at : at + column.shape[along]]
        finished.append(slab.reshape(*slab.shape[:along], *a.shape[along:]))
        at += column.shape[along]
    return tuple(finished)


def in_blocks(x, dim, peers):
    before, after = (x.shape[:dim], x.shape[dim + 1 :])
    return jnp.moveaxis(x.reshape(*before, peers, -1, *after), dim, 0)


def sum_at_owner(x, axis, dim):
    parts = in_blocks(x, dim, lax.axis_size(axis))
    arrived = lax.all_to_all(parts, axis, split_axis=0, concat_axis=0, tiled=True)
    return arrived.sum(axis=0)


def from_everyone(x, axis):
    copies = jnp.broadcast_to(x, (lax.axis_size(axis), *x.shape))
    return lax.all_to_all(copies, axis, split_axis=0, concat_axis=0, tiled=True)


def of_everyone(x, axis):
    everything = from_everyone(x, axis)
    return jnp.sum(everything, axis=0)


def supernode_pass(present, masked, listed_f, diag_part, ratio):
    row_block, row_listed = in_one_piece((masked, listed_f), "col", 0, 2)
    held = sum_at_owner(
        jnp.einsum("ij,ika->jka", present, row_block, precision=lax.Precision.HIGHEST), "row", 0
    )
    count_row = lax.axis_size("row")
    count_col = lax.axis_size("col")
    local_rows = held.shape[0]
    nodes = held.shape[1]
    narrow = held.shape[2] // count_col
    by_column = lax.all_to_all(held[None], "col", split_axis=3, concat_axis=0, tiled=True)
    grouped = by_column.reshape(count_row, 1, ratio, local_rows, nodes, narrow)
    moved = lax.all_to_all(grouped, "row", split_axis=0, concat_axis=1, tiled=True)
    ordered = jnp.transpose(moved[0], (1, 0, 2, 3, 4)).reshape(
        ratio * count_row * local_rows, nodes, narrow
    )
    summed = jnp.transpose(ordered, (2, 1, 0))
    columns = -summed * jnp.transpose(row_listed)[None, :, :]
    update = jnp.einsum("akj,jkb->akb", columns, row_block, precision=lax.Precision.HIGHEST)
    schur = diag_part - of_everyone(update, "row")
    return (columns, schur)


def local(inv_known, pattern, factor, listed, diag_inverse):
    tile = inv_known.shape[0] // pattern.shape[0]
    flags = pattern.astype(jnp.float32)
    spread = jnp.repeat(jnp.repeat(flags, tile, axis=0), tile, axis=1)
    present = inv_known * spread
    listed_f = listed.astype(jnp.float32)
    masked = factor * listed_f[:, :, None]
    ratio = lax.axis_size("col") // lax.axis_size("row")
    columns, schur = supernode_pass(present, masked, listed_f, diag_inverse, ratio)
    return (columns, schur)


def solution(mesh):
    in_specs = (
        P("row", "col"),
        P("row", "col"),
        P(("row", "col"), None, None),
        P(("row", "col"), None),
        P("col", None, None),
    )
    out_specs = (P("col", None, "row"), P("col", None, None))
    return jax.shard_map(local, mesh=mesh, in_specs=in_specs, out_specs=out_specs, check_vma=False)
```

profile of v0, /device:TPU:32, one launch (start us, length us, event | category | flops | bytes accessed | tf_op | source)
XLA Modules:
  0.0 265.9 jit_solution(16687229242903270589)
XLA Ops:
  7.2 0.7 fusion.8
  8.0 0.9 copy_multiply_fusion
  9.6 1.2 copy.47
  10.8 0.7 convert_element_type.6
  11.7 67.7 %all-gather.2.cloned.1.call-done = f32[512,2,513]{2,0,1:T(8,128)} async-done(((f32[16,2,513]{2,0,1:T(8,128)}), f32[512,2,513]{2,0,1:T(8,128)}) %all-gather.2.cloned.1.call-update) | async-done | bytes 2101264 | tf_op jit(solution)/shard_map/all_gather | solution.py:10
  79.4 3.5 %fusion.2 = f32[256,2,512]{2,0,1:T(8,128)S(1)} fusion(f32[512,2,513]{2,0,1:T(8,128)} %all-gather.2.cloned.1.call-done, f32[512,256]{0,1:T(8,128)S(1)} %bitcast_multiply_fusion), kind=kOutput, calls=%fused_computation.2 | convolution fusion | flops 1610612736 | bytes 3670016 | tf_op jit(solution)/shard_map/ij,ika->jka/dot_general | solution.py:42
  83.0 66.8 %all_to_all.34 = f32[16,16,2,512]{3,1,2,0:T(8,128)S(1)} all-to-all(f32[16,16,2,512]{3,1,2,0:T(8,128)S(1)} %copy.50), channel_id=1, replica_groups=mesh['row'=16,'col'=32] {'row'}, dimensions={0} | all-to-all | bytes 2097152 | tf_op jit(solution)/shard_map/all_to_all | solution.py:25
  150.1 0.7 reshape.37
  150.8 15.7 %all_to_all.35 = f32[32,1,512]{2,1,0:T(1,128)S(1)} all-to-all(f32[32,1,512]{2,1,0:T(1,128)S(1)} %reshape.37), channel_id=1, replica_groups=mesh['row'=16,'col'=32] {'col'}, dimensions={0} | all-to-all | bytes 131072 | tf_op jit(solution)/shard_map/all_to_all | solution.py:49
  167.0 0.8 reduce.2
  167.8 0.7 reshape.38
  168.5 1.2 copy.59
  169.8 1.3 copy.65
  171.1 0.9 reshape.39
  172.0 3.5 %all-to-all-start.2 = ((f32[16,1,1024]{2,1,0:T(1,128)}), f32[16,1,1024]{2,1,0:T(1,128)S(1)}, u32[]{:S(2)}, u32[]{:S(2)}) async-start(f32[16,1,1024]{2,1,0:T(1,128)} %reshape.39), calls=%async_computation.2 | async-start | bytes 131072 | tf_op jit(solution)/shard_map/all_to_all | solution.py:51
  175.7 16.0 %all-to-all-done.2 = f32[16,1,1024]{2,1,0:T(1,128)S(1)} async-done(((f32[16,1,1024]{2,1,0:T(1,128)}), f32[16,1,1024]{2,1,0:T(1,128)S(1)}, u32[]{:S(2)}, u32[]{:S(2)}) %all-to-all-start.2) | async-done | bytes 65568 | tf_op jit(solution)/shard_map/all_to_all | solution.py:51
  191.8 0.8 reduce.3
  192.8 0.8 negate_bitcast_fusion
  193.6 1.5 copy.55
  195.4 1.2 fusion.4
  196.6 1.1 broadcast_in_dim.20
  197.7 3.7 %all-to-all-start.3 = ((f32[16,16,2,512]{3,1,2,0:T(8,128)}), f32[16,16,2,512]{3,1,2,0:T(8,128)S(1)}, u32[]{:S(2)}, u32[]{:S(2)}) async-start(f32[16,16,2,512]{3,1,2,0:T(8,128)} %broadcast_in_dim.20), calls=%async_computation.3 | async-start | bytes 2097152 | tf_op jit(solution)/shard_map/all_to_all | solution.py:31
  201.4 0.7 copy.57
  202.0 56.3 %all-to-all-done.3 = f32[16,16,2,512]{3,1,2,0:T(8,128)S(1)} async-done(((f32[16,16,2,512]{3,1,2,0:T(8,128)}), f32[16,16,2,512]{3,1,2,0:T(8,128)S(1)}, u32[]{:S(2)}, u32[]{:S(2)}) %all-to-all-start.3) | async-done | bytes 1048608 | tf_op jit(solution)/shard_map/all_to_all | solution.py:31
  (22 shorter events, 3.3 us)
Async XLA Ops:
  7.2 72.3 %all-gather.2.cloned.1.call-start = ((), (), s32[]{:S(2)}) async-start(), calls=%async_computation.4 | async-start | bytes 2703360 | tf_op jit(solution)/shard_map/all_gather | solution.py:10
  149.8 25.7 %copy-start = (f32[512,2,513]{2,0,1:T(8,128)S(1)}, f32[512,2,513]{2,0,1:T(8,128)}, u32[]{:S(2)}) copy-start(f32[512,2,513]{2,0,1:T(8,128)} %all-gather.2.cloned.1.call-done) | copy-start | bytes 6303748
  172.0 19.8 %all-to-all-start.2 = ((f32[16,1,1024]{2,1,0:T(1,128)}), f32[16,1,1024]{2,1,0:T(1,128)S(1)}, u32[]{:S(2)}, u32[]{:S(2)}) async-start(f32[16,1,1024]{2,1,0:T(1,128)} %reshape.39), calls=%async_computation.2 | async-start | bytes 131072 | tf_op jit(solution)/shard_map/all_to_all | solution.py:51
  196.6 61.8 %copy-start.1 = (f32[16,2,512]{2,1,0:T(2,128)S(1)}, f32[16,2,512]{2,1,0:T(2,128)}, u32[]{:S(2)}) copy-start(f32[16,2,512]{2,1,0:T(2,128)} %param.9) | copy-start | bytes 196612
  197.7 60.6 %all-to-all-start.3 = ((f32[16,16,2,512]{3,1,2,0:T(8,128)}), f32[16,16,2,512]{3,1,2,0:T(8,128)S(1)}, u32[]{:S(2)}, u32[]{:S(2)}) async-start(f32[16,16,2,512]{3,1,2,0:T(8,128)} %broadcast_in_dim.20), calls=%async_computation.3 | async-start | bytes 2097152 | tf_op jit(solution)/shard_map/all_to_all | solution.py:31
Sparse Core Ops, SparseCore 0:
  10.1 69.3 all-gather.1
where the time goes:
time: 267 us; the launch traced here: 266 us
  waiting for transfers between devices  140 us (52%)
  blocking collectives  82.5 us (31%)
  between operations  14.2 us (5%)
  local copies, waits for them, and re-layouts  11.8 us (4%)
  starting transfers between devices  7.2 us (3%)
  other arithmetic  5.58 us (2%)
  matrix products  4.68 us (2%)
    all_gather x1, waiting for transfers between devices, in_one_piece(): lax.all_gather(both, axis, axis=dim, tiled=True)  67.7 us
    all_to_all x1, blocking collectives, sum_at_owner(): lax.all_to_all(parts, axis, split_axis=0, concat_axis=0, tiled=True)  66.8 us
    all_to_all x1, waiting for transfers between devices, from_everyone(): return lax.all_to_all(copies, axis, split_axis=0, concat_axis=0, tiled=True)  56.3 us
    all_to_all x1, waiting for transfers between devices, supernode_pass(): lax.all_to_all(grouped, 'row', split_axis=0, concat_axis=1, tiled=True)  16 us
    all_to_all x1, blocking collectives, supernode_pass(): lax.all_to_all(held[None], 'col', split_axis=3, concat_axis=0, tiled=True)  15.7 us
  transfers between devices with their start and end apart: 3, of which 3 were waited for; matrix products, arithmetic and copies ran while one was open for 1% of the time, Pallas kernels for 0%

commit v1 on v0

--- a/solution.py
+++ b/solution.py
@@ -2,6 +2,12 @@
 import jax.numpy as jnp
 from jax import lax
 from jax.sharding import PartitionSpec as P
+
+
+def exchange_blocks(array, axis, split, join):
+    pieces = jnp.split(array, lax.axis_size(axis), axis=split)
+    received = lax.all_to_all(jnp.stack(pieces), axis, 0, 0)
+    return jnp.concatenate(received, axis=join)
 
 
 def in_one_piece(arrays, axis, dim, along):
@@ -46,7 +52,7 @@
     local_rows = held.shape[0]
     nodes = held.shape[1]
     narrow = held.shape[2] // count_col
-    by_column = lax.all_to_all(held[None], "col", split_axis=3, concat_axis=0, tiled=True)
+    by_column = exchange_blocks(held[None], "col", 3, 0)
     grouped = by_column.reshape(count_row, 1, ratio, local_rows, nodes, narrow)
     moved = lax.all_to_all(grouped, "row", split_axis=0, concat_axis=1, tiled=True)
     ordered = jnp.transpose(moved[0], (1, 0, 2, 3, 4)).reshape(

time: 267 us -> 266 us (level)
    unnamed x11 -> x42, local copies, waits for them, and re-layouts: 5.09 us -> 6.1 us
where the time goes in v1:
time: 266 us
  waiting for transfers between devices  140 us (53%)
  blocking collectives  82.6 us (31%)
  between operations  14.2 us (5%)
  local copies, waits for them, and re-layouts  10.1 us (4%)
  starting transfers between devices  7.2 us (3%)
  other arithmetic  6.96 us (3%)
  matrix products  4.68 us (2%)
    all_gather x1, waiting for transfers between devices, in_one_piece(): lax.all_gather(both, axis, axis=dim, tiled=True)  67.7 us
    all_to_all x1, blocking collectives, sum_at_owner(): lax.all_to_all(parts, axis, split_axis=0, concat_axis=0, tiled=True)  66.9 us
    all_to_all x1, waiting for transfers between devices, from_everyone(): return lax.all_to_all(copies, axis, split_axis=0, concat_axis=0, tiled=True)  56.3 us
    all_to_all x1, waiting for transfers between devices, supernode_pass(): lax.all_to_all(grouped, 'row', split_axis=0, concat_axis=1, tiled=True)  16 us
    all_to_all x1, blocking collectives, exchange_blocks(): received = lax.all_to_all(jnp.stack(pieces), axis, 0, 0)  15.7 us
    unnamed x42, local copies, waits for them, and re-layouts  6.1 us
  transfers between devices with their start and end apart: 3, of which 3 were waited for; matrix products, arithmetic and copies ran while one was open for 1% of the time, Pallas kernels for 0%

profile of v1, /device:TPU:32, one launch (start us, length us, event | category | flops | bytes accessed | tf_op | source)
XLA Modules:
  0.0 265.7 jit_solution(16776627218916270705)
XLA Ops:
  7.2 0.7 fusion.8
  8.0 0.9 copy_multiply_fusion
  8.9 0.6 pad_maximum_fusion
  9.6 1.2 copy.94
  10.8 0.7 convert_element_type.6
  11.7 67.7 %all-gather.2.cloned.1.call-done = f32[512,2,513]{2,0,1:T(8,128)} async-done(((f32[16,2,513]{2,0,1:T(8,128)}), f32[512,2,513]{2,0,1:T(8,128)}) %all-gather.2.cloned.1.call-update) | async-done | bytes 2101264 | tf_op jit(solution)/shard_map/all_gather | solution.py:16
  79.4 3.5 %fusion.2 = f32[256,2,512]{2,0,1:T(8,128)S(1)} fusion(f32[512,2,513]{2,0,1:T(8,128)} %all-gather.2.cloned.1.call-done, f32[512,256]{0,1:T(8,128)S(1)} %bitcast_multiply_fusion), kind=kOutput, calls=%fused_computation.2 | convolution fusion | flops 1610612736 | bytes 3670016 | tf_op jit(solution)/shard_map/ij,ika->jka/dot_general | solution.py:48
  83.0 66.9 %all_to_all.24 = f32[16,16,2,512]{3,1,2,0:T(8,128)} all-to-all(f32[16,16,2,512]{3,1,2,0:T(8,128)S(1)} %copy.97), channel_id=1, replica_groups=mesh['row'=16,'col'=32] {'row'}, dimensions={0} | all-to-all | bytes 2097152 | tf_op jit(solution)/shard_map/all_to_all | solution.py:31
  149.9 1.4 reduce_sum.18
  153.7 15.7 %all_to_all.25 = f32[32,1,512]{2,1,0:T(1,128)S(1)} all-to-all(f32[32,1,512]{2,1,0:T(1,128)S(1)} %reshape.32), channel_id=1, replica_groups=mesh['row'=16,'col'=32] {'col'}, dimensions={0} | all-to-all | bytes 131072 | tf_op jit(solution)/shard_map/all_to_all | solution.py:9
  169.4 0.5 broadcast.3
  169.9 0.8 reduce.2
  170.9 0.9 reshape.34
  171.8 3.5 %all-to-all-start.2 = ((f32[16,1,1024]{2,1,0:T(1,128)}), f32[16,1,1024]{2,1,0:T(1,128)S(1)}, u32[]{:S(2)}, u32[]{:S(2)}) async-start(f32[16,1,1024]{2,1,0:T(1,128)} %reshape.34), calls=%async_computation.2 | async-start | bytes 131072 | tf_op jit(solution)/shard_map/all_to_all | solution.py:57
  175.5 16.0 %all-to-all-done.2 = f32[16,1,1024]{2,1,0:T(1,128)S(1)} async-done(((f32[16,1,1024]{2,1,0:T(1,128)}), f32[16,1,1024]{2,1,0:T(1,128)S(1)}, u32[]{:S(2)}, u32[]{:S(2)}) %all-to-all-start.2) | async-done | bytes 65568 | tf_op jit(solution)/shard_map/all_to_all | solution.py:57
  191.5 0.8 reduce.3
  192.6 0.8 negate_bitcast_fusion
  193.4 1.5 copy.99
  195.2 1.2 fusion.4
  196.4 1.1 broadcast_in_dim.20
  197.5 3.7 %all-to-all-start.3 = ((f32[16,16,2,512]{3,1,2,0:T(8,128)}), f32[16,16,2,512]{3,1,2,0:T(8,128)S(1)}, u32[]{:S(2)}, u32[]{:S(2)}) async-start(f32[16,16,2,512]{3,1,2,0:T(8,128)} %broadcast_in_dim.20), calls=%async_computation.3 | async-start | bytes 2097152 | tf_op jit(solution)/shard_map/all_to_all | solution.py:37
  201.2 0.7 copy.101
  201.8 56.3 %all-to-all-done.3 = f32[16,16,2,512]{3,1,2,0:T(8,128)S(1)} async-done(((f32[16,16,2,512]{3,1,2,0:T(8,128)}), f32[16,16,2,512]{3,1,2,0:T(8,128)S(1)}, u32[]{:S(2)}, u32[]{:S(2)}) %all-to-all-start.3) | async-done | bytes 1048608 | tf_op jit(solution)/shard_map/all_to_all | solution.py:37
  258.2 0.7 copy.102
  (51 shorter events, 3.7 us)
Async XLA Ops:
  7.2 72.3 %all-gather.2.cloned.1.call-start = ((), (), s32[]{:S(2)}) async-start(), calls=%async_computation.4 | async-start | bytes 2703360 | tf_op jit(solution)/shard_map/all_gather | solution.py:16
  149.9 25.4 %copy-start = (f32[512,2,513]{2,0,1:T(8,128)S(1)}, f32[512,2,513]{2,0,1:T(8,128)}, u32[]{:S(2)}) copy-start(f32[512,2,513]{2,0,1:T(8,128)} %all-gather.2.cloned.1.call-done) | copy-start | bytes 6303748
  171.8 19.8 %all-to-all-start.2 = ((f32[16,1,1024]{2,1,0:T(1,128)}), f32[16,1,1024]{2,1,0:T(1,128)S(1)}, u32[]{:S(2)}, u32[]{:S(2)}) async-start(f32[16,1,1024]{2,1,0:T(1,128)} %reshape.34), calls=%async_computation.2 | async-start | bytes 131072 | tf_op jit(solution)/shard_map/all_to_all | solution.py:57
  196.4 61.8 %copy-start.1 = (f32[16,2,512]{2,1,0:T(2,128)S(1)}, f32[16,2,512]{2,1,0:T(2,128)}, u32[]{:S(2)}) copy-start(f32[16,2,512]{2,1,0:T(2,128)} %param.9) | copy-start | bytes 196612
  197.5 60.6 %all-to-all-start.3 = ((f32[16,16,2,512]{3,1,2,0:T(8,128)}), f32[16,16,2,512]{3,1,2,0:T(8,128)S(1)}, u32[]{:S(2)}, u32[]{:S(2)}) async-start(f32[16,16,2,512]{3,1,2,0:T(8,128)} %broadcast_in_dim.20), calls=%async_computation.3 | async-start | bytes 2097152 | tf_op jit(solution)/shard_map/all_to_all | solution.py:37
Sparse Core Ops, SparseCore 0:
  10.1 69.3 all-gather.1
